TPU v7x, 32 devices: a whole 2x2x4 slice. The times are simulated.
32 devices in a mesh: group: 8 (over z, x), fsdp: 4 (over y, core).
Axes of the slice: x: 2, y: 2, z: 4, core: 2. Of those that a mesh axis runs over, the one named last changes fastest.
Arguments:
- mol_qkv: bfloat16 [64, 128, 3, 4096], P('group', None, None, 'fsdp'), may hold values from -12 to 12
- pair_list: int32 [128, 3], replicated, may hold values from 0 to 7, as said below
- head_proj: bfloat16 [32, 128, 256], P('fsdp'), may hold values from -0.5 to 0.5
- head_out: float32 [32, 256], P('fsdp'), may hold values from -0.375 to 0.375
- labels: int32 [128], P('group'), may hold values 0 or 1
Outputs:
- mol_grad: bfloat16 [64, 128, 3, 4096], P('group', None, None, 'fsdp')
- pair_logits: float32 [128], P('group')
- mean_loss: float32 [], replicated
Inputs may be any that keep to these rules, and one draw needn't show every extreme that they name: `pair_list`: pair p belongs to owner p // 16; column 0 is the first molecule's index among the owner's 8 molecules, column 1 the group index that holds the second molecule, column 2 its index among that holder's 8 molecules; molecule m is held by group m // 8. `pair_list`: among one owner's pairs, at most 4 take their second molecule from any one holder, and those name at most 2 different molecules; every owner reaches both bounds.
All inputs are finite; a program needn't handle non-finite values. No bound on the sum of `labels` on one device may be relied on, other than what follows from the above.
Results may differ from a plain program's by a relative error of at most 0.0075.
Values may be sent and summed in bfloat16 or wider, within the bound.
A program may use at most 192 MiB of HBM per device.

v0:
```python
import jax
import jax.numpy as jnp
from jax import lax
from jax.sharding import PartitionSpec as P

loss_scale = 8192.0


def split_heads(rows_in, component, heads, head_dim):
    return rows_in[:, :, component].reshape(rows_in.shape[0], rows_in.shape[1], heads, head_dim)


def forward(query_rows, key_rows, value_rows, head_proj, head_out, inv_root, length):
    scores = (
        jnp.einsum("plhd,pmhd->phlm", query_rows, key_rows, preferred_element_type=jnp.float32)
        * inv_root
    )
    row_max = jnp.max(scores, axis=-1, keepdims=True)
    lifted = jnp.exp(scores - row_max)
    attn_weights = lifted / jnp.sum(lifted, axis=-1, keepdims=True)
    weights_bf = attn_weights.astype(jnp.bfloat16)
    context = jnp.einsum(
        "phlm,pmhd->plhd", weights_bf, value_rows, preferred_element_type=jnp.float32
    ).astype(jnp.bfloat16)
    hidden = jnp.einsum("plhd,hdr->plhr", context, head_proj, preferred_element_type=jnp.float32)
    partial_value = jnp.sum(jax.nn.silu(hidden) * head_out[None, None], axis=(1, 2, 3)) / length
    return (partial_value, (attn_weights, weights_bf, hidden))


def backward(
    query_rows, key_rows, value_rows, head_proj, head_out, saved, grad_out, inv_root, length
):
    attn_weights, weights_bf, hidden = saved
    sigmoid_h = jax.nn.sigmoid(hidden)
    silu_slope = sigmoid_h * (1.0 + hidden * (1.0 - sigmoid_h))
    dhidden = (grad_out[:, None, None, None] / length * head_out[None, None] * silu_slope).astype(
        jnp.bfloat16
    )
    dcontext = jnp.einsum(
        "plhr,hdr->plhd", dhidden, head_proj, preferred_element_type=jnp.float32
    ).astype(jnp.bfloat16)
    dvalues = jnp.einsum(
        "phlm,plhd->pmhd", weights_bf, dcontext, preferred_element_type=jnp.float32
    )
    dweights = jnp.einsum(
        "plhd,pmhd->phlm", dcontext, value_rows, preferred_element_type=jnp.float32
    )
    dscores = (
        attn_weights
        * (dweights - jnp.sum(dweights * attn_weights, axis=-1, keepdims=True))
        * inv_root
    ).astype(jnp.bfloat16)
    dqueries = jnp.einsum("phlm,pmhd->plhd", dscores, key_rows, preferred_element_type=jnp.float32)
    dkey_rows = jnp.einsum(
        "phlm,plhd->pmhd", dscores, query_rows, preferred_element_type=jnp.float32
    )
    return (dqueries, dkey_rows, dvalues)


def routing(blocks, mol_count, capacity, device):
    groups, per_owner, _ = blocks.shape
    holder = blocks[:, :, 1]
    member = blocks[:, :, 2]
    position = jnp.arange(per_owner, dtype=jnp.int32)
    mol_key = holder * mol_count + member
    matches = mol_key[:, :, None] == mol_key[:, None, :]
    earlier = matches & (position[None, None, :] < position[None, :, None])
    leading = jnp.logical_not(jnp.any(earlier, axis=2))
    leader = jnp.argmax(matches, axis=2)
    per_holder = (
        (holder[:, :, None] == jnp.arange(groups, dtype=jnp.int32)[None, None, :])
        & leading[:, :, None]
    ).astype(jnp.int32)
    rank_all = jnp.cumsum(per_holder, axis=1) - per_holder
    rank_in = jnp.take_along_axis(rank_all, holder[:, :, None], axis=2)[:, :, 0]
    slot_index = holder * capacity + rank_in
    return_slot = jnp.take_along_axis(slot_index, leader, axis=1)
    to_device = leading & (holder == device)
    picked = to_device[:, :, None] & (
        rank_in[:, :, None] == jnp.arange(capacity, dtype=jnp.int32)[None, None, :]
    )
    send_member = jnp.sum(picked.astype(jnp.int32) * member[:, :, None], axis=1)
    send_valid = jnp.any(picked, axis=1)
    return (return_slot, return_slot, send_member, send_valid)


def local(mol_qkv, pair_list, head_proj, head_out, labels):
    groups = lax.axis_size("group")
    device = lax.axis_index("group")
    mol_count, length, _, row_width = mol_qkv.shape
    heads_here, head_dim, inner_width = head_proj.shape
    total_pairs = pair_list.shape[0]
    per_owner = total_pairs // groups
    inv_root = head_dim ** (-0.5)
    blocks = pair_list.reshape(groups, per_owner, 3)
    capacity = per_owner // groups
    fetch_slot, return_slot, send_member, send_valid = routing(blocks, mol_count, capacity, device)
    slots_all = groups * capacity
    flat_member = send_member.reshape(slots_all)
    flat_valid = send_valid.reshape(slots_all)
    outgoing = jnp.take(mol_qkv, flat_member, axis=0)
    outgoing = jnp.where(flat_valid[:, None, None, None], outgoing, jnp.zeros_like(outgoing))
    incoming = lax.all_to_all(outgoing, "group", split_axis=0, concat_axis=0, tiled=True)
    my_pairs = lax.dynamic_index_in_dim(blocks, device, 0, keepdims=False)
    my_fetch = lax.dynamic_index_in_dim(fetch_slot, device, 0, keepdims=False)
    my_return = lax.dynamic_index_in_dim(return_slot, device, 0, keepdims=False)
    partner_rows = jnp.take(incoming, my_fetch, axis=0)
    own_rows = jnp.take(mol_qkv, my_pairs[:, 0], axis=0)
    qa, ka, va = [split_heads(own_rows, c, heads_here, head_dim) for c in range(3)]
    qb, kb, vb = [split_heads(partner_rows, c, heads_here, head_dim) for c in range(3)]
    part_ab, saved_ab = forward(qa, kb, vb, head_proj, head_out, inv_root, length)
    part_ba, saved_ba = forward(qb, ka, va, head_proj, head_out, inv_root, length)
    logits = lax.psum(part_ab + part_ba, "fsdp")
    targets = labels.astype(jnp.float32)
    loss_terms = jax.nn.softplus(logits) - targets * logits
    loss_sum = lax.psum(jnp.sum(loss_terms), "group")
    mean_loss = loss_sum / total_pairs
    grad_out = (jax.nn.sigmoid(logits) - targets) * loss_scale
    dq_a, dk_b, dv_b = backward(
        qa, kb, vb, head_proj, head_out, saved_ab, grad_out, inv_root, length
    )
    dq_b, dk_a, dv_a = backward(
        qb, ka, va, head_proj, head_out, saved_ba, grad_out, inv_root, length
    )
    grad_first = jnp.stack([dq_a, dk_a, dv_a], axis=2).reshape(per_owner, -1)
    grad_second = jnp.stack([dq_b, dk_b, dv_b], axis=2).reshape(per_owner, -1)
    own_pick = (my_pairs[:, 0][None, :] == jnp.arange(mol_count, dtype=jnp.int32)[:, None]).astype(
        jnp.float32
    )
    own_sum = jnp.dot(
        own_pick, grad_first, precision=lax.Precision.HIGHEST, preferred_element_type=jnp.float32
    )
    back_pick = (my_return[None, :] == jnp.arange(slots_all, dtype=jnp.int32)[:, None]).astype(
        jnp.float32
    )
    outgoing_grad = jnp.dot(
        back_pick, grad_second, precision=lax.Precision.HIGHEST, preferred_element_type=jnp.float32
    )
    outgoing_grad = outgoing_grad.astype(jnp.bfloat16).reshape(slots_all, length, 3, row_width)
    returned = lax.all_to_all(outgoing_grad, "group", split_axis=0, concat_axis=0, tiled=True)
    land_pick = (
        (flat_member[None, :] == jnp.arange(mol_count, dtype=jnp.int32)[:, None])
        & flat_valid[None, :]
    ).astype(jnp.bfloat16)
    partner_sum = jnp.dot(
        land_pick, returned.reshape(slots_all, -1), preferred_element_type=jnp.float32
    )
    mol_grad = (own_sum + partner_sum).astype(jnp.bfloat16).reshape(mol_qkv.shape)
    return (mol_grad, logits, mean_loss)


def solution(mesh):
    placed = (
        P("group", None, None, "fsdp"),
        P(),
        P("fsdp", None, None),
        P("fsdp", None),
        P("group"),
    )
    return jax.shard_map(
        local,
        mesh=mesh,
        in_specs=placed,
        out_specs=(P("group", None, None, "fsdp"), P("group"), P()),
        check_vma=False,
    )
```

profile of v0, /device:TPU:8, one launch (start us, length us, event | category | flops | bytes accessed | tf_op | source)
XLA Modules:
  0.0 1073.1 jit_solution(13335378748333062560)
XLA Ops:
  13.5 10.9 %select_select_fusion = bf16[16,128,3,1024]{3,1,2,0:T(8,128)(2,1)} fusion(bf16[16,128,3,1024]{3,1,2,0:T(8,128)(2,1)} %gather_fusion.3, pred[16]{0:T(512)(128)(4,1)S(1)} %get-tuple-element.46, pred[16]{0:T(512)(128)(4,1)S(1)} %broadcast_in_dim.42), kind=kLoop, calls=%fused_computation.43 | loop fusion | flops 12582912 | bytes 25165856 | tf_op jit(solution)/shard_map/jit(_where)/select_n | solution.py:102
  72.9 228.1 %all-to-all-done = bf16[16,128,3,1024]{3,1,2,0:T(8,128)(2,1)} async-done(((bf16[16,128,3,1024]{3,1,2,0:T(8,128)(2,1)}), bf16[16,128,3,1024]{3,1,2,0:T(8,128)(2,1)}, u32[]{:S(2)}, u32[]{:S(2)}) %all-to-all-start) | async-done | bytes 12582944 | tf_op jit(solution)/shard_map/all_to_all | solution.py:103
  301.0 11.1 %gather_fusion = bf16[16,128,3,1024]{3,1,2,0:T(8,128)(2,1)} fusion(bf16[16,128,3,1024]{3,1,2,0:T(8,128)(2,1)} %all-to-all-done, s32[1024]{0:T(1024)S(1)} %pad_clamp_fusion.1), kind=kCustom, calls=%fused_computation.2 | custom fusion | bytes 25165888 | tf_op jit(solution)/shard_map/jit(_take)/gather | solution.py:107
  342.8 9.9 fusion.172
  362.6 10.4 fusion.60
  373.0 19.0 %fusion.14 = (f32[16]{0:T(128)S(1)}, f32[16]{0:T(128)S(1)}, f32[8,16,128,256]{3,2,1,0:T(8,128)}) fusion(f32[8,256]{1,0:T(8,128)S(1)} %copy-done.6, f32[8,16,128,256]{3,2,1,0:T(8,128)} %fusion.60, bf16[8,128,256]{2,1,0:T(8,128)(2,1)S(1)} %copy-done, bf16[16,128,8,128]{1,3,2,0:T(8,128)(2,1)} %bitcast.196, f32[16,8,128,128]{2,3,1,0:T(8,128)} %get-tuple-element.42, ...), kind=kOutput, calls=%fused_computation.26 | convolution fusion | flops 1667235840 | bytes 46735488 | tf_op jit(solution)/shard_map/plhd,hdr->plhr/dot_general | solution.py:25
  425.8 10.3 convert_bitcast_fusion
  444.4 18.0 %fusion.101 = f32[16,128,1,8,128]{1,4,3,0,2:T(8,128)} fusion(bf16[16,128,8,128]{1,3,2,0:T(8,128)(2,1)} %bitcast.195, f32[16,8,128,128]{2,3,1,0:T(8,128)} %fusion.76, f32[16,8,128,128]{2,3,1,0:T(8,128)} %get-tuple-element.42, f32[16,8,128]{2,1,0:T(8,128)S(1)} %get-tuple-element.41), kind=kOutput, calls=%fused_computation.95 | convolution fusion | flops 551567488 | bytes 29425664 | tf_op jit(solution)/shard_map/phlm,pmhd->plhd/dot_general | solution.py:53
  462.4 18.1 %fusion.107 = f32[16,128,1,8,128]{1,4,3,0,2:T(8,128)} fusion(bf16[16,128,8,128]{1,3,2,0:T(8,128)(2,1)} %bitcast.193, f32[16,8,128,128]{2,3,1,0:T(8,128)} %fusion.80, f32[16,8,128,128]{2,3,1,0:T(8,128)} %get-tuple-element.44, f32[16,8,128]{2,1,0:T(8,128)S(1)} %get-tuple-element.43), kind=kOutput, calls=%fused_computation.97 | convolution fusion | flops 551567488 | bytes 29425664 | tf_op jit(solution)/shard_map/phlm,plhd->pmhd/dot_general | solution.py:54
  480.4 18.7 %pad_maximum_fusion.1 = f32[16,128,3,8,128]{1,4,3,0,2:T(8,128)} fusion(f32[16,128,1,8,128]{1,4,3,0,2:T(8,128)} %fusion.110, f32[16,128,1,8,128]{1,4,3,0,2:T(8,128)} %fusion.107, f32[16,128,1,8,128]{1,4,3,0,2:T(8,128)} %fusion.101), kind=kLoop, calls=%fused_computation.18 | loop fusion | flops 12582912 | bytes 50331648 | tf_op jit(solution)/shard_map/stack | solution.py:126
  499.1 24.7 %copy.147 = f32[16,128,3,8,128]{4,3,2,1,0:T(8,128)} copy(f32[16,128,3,8,128]{1,4,3,0,2:T(8,128)} %pad_maximum_fusion.1) | data formatting | bytes 50331648 | tf_op jit(solution)/shard_map/stack | solution.py:126
  523.8 34.5 %convolution_convert_fusion = bf16[16,393216]{1,0:T(8,128)(2,1)} fusion(f32[2,8,3072,128]{3,2,1,0:T(8,128)} %bitcast.189, s32[16]{0:T(128)S(1)} %copy-done.10), kind=kOutput, calls=%fused_computation.9 | convolution fusion | flops 1214251264 | bytes 37748800 | tf_op jit(solution)/shard_map/dot_general | solution.py:136
  558.3 30.0 %reshape.150 = bf16[16,128,3,1024]{3,2,1,0:T(4,128)(2,1)} reshape(bf16[16,393216]{1,0:T(8,128)(2,1)} %convolution_convert_fusion) | data formatting | bytes 25165824 | tf_op jit(solution)/shard_map/reshape | solution.py:139
  588.3 12.2 %copy.148 = bf16[16,128,3,1024]{3,1,2,0:T(8,128)(2,1)} copy(bf16[16,128,3,1024]{3,2,1,0:T(4,128)(2,1)} %reshape.150) | data formatting | bytes 25165824 | tf_op jit(solution)/shard_map/reshape | solution.py:139
  607.8 281.0 %psum.15 = f32[]{:T(128)} all-reduce(f32[]{:T(128)} %get-tuple-element.39), channel_id=1, replica_groups=mesh['group'=8,'fsdp'=4] {'group'}, use_global_device_ids=true, to_apply=%region_15.17 | all-reduce | flops 1 | bytes 8 | tf_op jit(solution)/shard_map/psum | solution.py:116
  888.8 18.1 %fusion.98 = f32[16,128,1,8,128]{1,4,3,0,2:T(8,128)} fusion(bf16[16,128,8,128]{1,3,2,0:T(8,128)(2,1)} %bitcast.199, f32[16,8,128,128]{2,3,1,0:T(8,128)} %fusion.76, f32[16,8,128,128]{2,3,1,0:T(8,128)} %get-tuple-element.42, f32[16,8,128]{2,1,0:T(8,128)S(1)} %get-tuple-element.41), kind=kOutput, calls=%fused_computation.94 | convolution fusion | flops 551567488 | bytes 29425664 | tf_op jit(solution)/shard_map/phlm,plhd->pmhd/dot_general | solution.py:54
  906.9 17.9 %fusion.104 = f32[16,128,1,8,128]{1,4,3,0,2:T(8,128)} fusion(bf16[16,128,8,128]{1,3,2,0:T(8,128)(2,1)} %bitcast.201, f32[16,8,128,128]{2,3,1,0:T(8,128)} %fusion.80, f32[16,8,128,128]{2,3,1,0:T(8,128)} %get-tuple-element.44, f32[16,8,128]{2,1,0:T(8,128)S(1)} %get-tuple-element.43), kind=kOutput, calls=%fused_computation.96 | convolution fusion | flops 551567488 | bytes 29425664 | tf_op jit(solution)/shard_map/phlm,pmhd->plhd/dot_general | solution.py:53
  924.8 11.1 %fusion.113 = f32[16,128,1,8,128]{1,4,3,0,2:T(8,128)} fusion(bf16[16,128,8,128]{3,1,0,2:T(8,128)(2,1)} %copy-done.5, f32[16,8,128,128]{2,3,1,0:T(8,128)} %get-tuple-element.42, f32[16,8,128]{2,1,0:T(8,128)S(1)} %get-tuple-element.41), kind=kOutput, calls=%fused_computation.99 | convolution fusion | flops 541065216 | bytes 21037056 | tf_op jit(solution)/shard_map/phlm,plhd->pmhd/dot_general | solution.py:42
  935.9 15.5 %pad_maximum_fusion = f32[16,128,3,8,128]{1,4,3,0,2:T(8,128)} fusion(f32[16,128,1,8,128]{1,4,3,0,2:T(8,128)} %fusion.113, f32[16,128,1,8,128]{1,4,3,0,2:T(8,128)S(1)} %copy-done.4, f32[16,128,1,8,128]{1,4,3,0,2:T(8,128)} %fusion.104), kind=kLoop, calls=%fused_computation.17 | loop fusion | flops 12582912 | bytes 50331648 | tf_op jit(solution)/shard_map/stack | solution.py:125
  951.3 24.8 %copy.142 = f32[16,128,3,8,128]{4,3,2,1,0:T(8,128)} copy(f32[16,128,3,8,128]{1,4,3,0,2:T(8,128)} %pad_maximum_fusion) | data formatting | bytes 50331648 | tf_op jit(solution)/shard_map/stack | solution.py:125
  976.8 31.1 %fusion.7 = f32[8,393216]{1,0:T(8,128)} fusion(f32[2,8,3072,128]{3,2,1,0:T(8,128)} %bitcast.190, s32[16]{0:T(128)S(1)} %slice_bitcast_fusion.2), kind=kOutput, calls=%fused_computation.14 | convolution fusion | flops 603979904 | bytes 37748800 | tf_op jit(solution)/shard_map/dot_general | solution.py:130
  1007.9 18.7 %copy.149 = bf16[16,128,3,1024]{3,2,1,0:T(4,128)(2,1)} copy(bf16[16,128,3,1024]{3,1,2,0:T(8,128)(2,1)} %all-to-all-done.1) | data formatting | bytes 25165824 | tf_op jit(solution)/shard_map/all_to_all | solution.py:140
  1026.6 28.8 %reshape.151 = bf16[16,393216]{1,0:T(8,128)(2,1)} reshape(bf16[16,128,3,1024]{3,2,1,0:T(4,128)(2,1)} %copy.149) | data formatting | bytes 25165824 | tf_op jit(solution)/shard_map/reshape | solution.py:146
  1055.4 10.0 fusion.4
  (95 shorter events, 157.3 us)
Async XLA Ops:
  0.6 362.0 %copy-start = (bf16[8,128,256]{2,1,0:T(8,128)(2,1)S(1)}, bf16[8,128,256]{2,1,0:T(8,128)(2,1)}, u32[]{:S(2)}) copy-start(bf16[8,128,256]{2,1,0:T(8,128)(2,1)} %param.9) | copy-start | bytes 1572868
  1.8 11.7 %copy-start.9 = (s32[1,16,3]{1,2,0:T(4,128)}, s32[1,16,3]{1,2,0:T(4,128)S(1)}, u32[]{:S(2)}) copy-start(s32[1,16,3]{1,2,0:T(4,128)S(1)} %copy.226) | copy-start | bytes 580
  4.1 9.4 copy-start.11
  4.3 9.3 copy-start.7
  24.4 276.6 %all-to-all-start = ((bf16[16,128,3,1024]{3,1,2,0:T(8,128)(2,1)}), bf16[16,128,3,1024]{3,1,2,0:T(8,128)(2,1)}, u32[]{:S(2)}, u32[]{:S(2)}) async-start(bf16[16,128,3,1024]{3,1,2,0:T(8,128)(2,1)} %select_select_fusion), calls=%async_computation | async-start | bytes 25165824 | tf_op jit(solution)/shard_map/all_to_all | solution.py:103
  362.6 10.4 copy-start.6
  373.0 26.1 %copy-start.13 = (s32[16]{0:T(128)S(1)}, s32[16]{0:T(128)}, u32[]{:S(2)}) copy-start(s32[16]{0:T(128)} %param.11) | copy-start | bytes 196
  399.1 10.6 copy-start.14
  399.8 9.9 copy-start.3
  425.8 12.3 %copy-start.2 = (bf16[16,128,1,1024]{1,3,0,2:T(8,128)(2,1)S(1)}, bf16[16,128,1,1024]{1,3,0,2:T(8,128)(2,1)}, u32[]{:S(2)}) copy-start(bf16[16,128,1,1024]{1,3,0,2:T(8,128)(2,1)} %copy.126) | copy-start | bytes 12582916
  436.1 2.0 copy-start.5
  499.1 24.7 %copy-start.10 = (s32[16]{0:T(128)S(1)}, s32[16]{0:T(128)}, u32[]{:S(2)}) copy-start(s32[16]{0:T(128)} %get-tuple-element.26) | copy-start | bytes 196
  600.5 407.3 %all-to-all-start.1 = ((bf16[16,128,3,1024]{3,1,2,0:T(8,128)(2,1)}), bf16[16,128,3,1024]{3,1,2,0:T(8,128)(2,1)}, u32[]{:S(2)}, u32[]{:S(2)}) async-start(bf16[16,128,3,1024]{3,1,2,0:T(8,128)(2,1)} %copy.148), calls=%async_computation.1 | async-start | bytes 25165824 | tf_op jit(solution)/shard_map/all_to_all | solution.py:140
  924.8 11.1 %copy-start.4 = (f32[16,128,1,8,128]{1,4,3,0,2:T(8,128)S(1)}, f32[16,128,1,8,128]{1,4,3,0,2:T(8,128)}, u32[]{:S(2)}) copy-start(f32[16,128,1,8,128]{1,4,3,0,2:T(8,128)} %fusion.98) | copy-start | bytes 25165828
  1026.6 28.8 %copy-start.8 = (s32[16]{0:T(128)S(1)}, s32[16]{0:T(128)}, u32[]{:S(2)}) copy-start(s32[16]{0:T(128)} %copy-done.7) | copy-start | bytes 196
  1026.6 28.8 %copy-start.12 = (pred[16]{0:T(512)(128)(4,1)S(1)}, pred[16]{0:T(512)(128)(4,1)}, u32[]{:S(2)}) copy-start(pred[16]{0:T(512)(128)(4,1)} %copy-done.11) | copy-start | bytes 52
  1055.4 16.3 %copy-start.1 = (bf16[8,128,256]{2,1,0:T(8,128)(2,1)S(1)}, bf16[8,128,256]{2,1,0:T(8,128)(2,1)}, u32[]{:S(2)}) copy-start(bf16[8,128,256]{2,1,0:T(8,128)(2,1)} %param.9) | copy-start | bytes 1572868
where the time goes:
time: 1080 us; the launch traced here: 1070 us
  blocking collectives  288 us (27%)
  matrix products  250 us (23%)
  local copies, waits for them, and re-layouts  230 us (21%)
  waiting for transfers between devices  228 us (21%)
  other arithmetic  61.2 us (6%)
  starting transfers between devices  12.7 us (1%)
    psum x1, blocking collectives, local(): loss_sum = lax.psum(jnp.sum(loss_terms), 'group')  281 us
    all_to_all x1, waiting for transfers between devices, local(): lax.all_to_all(outgoing, 'group', split_axis=0, concat_axis=0, tiled=True)  228 us
    slice x8, local copies, waits for them, and re-layouts, split_heads(): rows_in[:, :, component]  48.1 us
    reshape x2, local copies, waits for them, and re-layouts, local(): outgoing_grad.astype(jnp.bfloat16).reshape(slots_all, length, 3, row_width)  42.3 us
    dot_general x2, matrix products, backward(): jnp.einsum('phlm,plhd->pmhd', dscores, query_rows, preferred_element_type...  36.2 us
    dot_general x2, matrix products, backward(): jnp.einsum('phlm,pmhd->plhd', dscores, key_rows, preferred_element_type=j...  35.9 us
    dot_general x1, matrix products, local(): jnp.dot(back_pick, grad_second, precision=lax.Precision.HIGHEST, preferre...  34.5 us
    dot_general x1, matrix products, local(): jnp.dot(own_pick, grad_first, precision=lax.Precision.HIGHEST, preferred_...  31.1 us
  transfers between devices with their start and end apart: 2, of which 1 were waited for; matrix products, arithmetic and copies ran while one was open for 15% of the time, Pallas kernels for 0%

commit v1 on v0

v1 whole, which is shorter than its diff:
```python
import functools

import jax
import jax.numpy as jnp
from jax import lax
from jax.experimental import pallas as pl
from jax.experimental.pallas import tpu as pltpu
from jax.sharding import PartitionSpec as P

loss_scale = 8192.0
chunks = 2
row_block = 16

NN = (((1,), (0,)), ((), ()))
NT = (((1,), (1,)), ((), ()))
TN = (((0,), (0,)), ((), ()))


def mm(a, b, dims):
    return lax.dot_general(a, b, dims, preferred_element_type=jnp.float32)


def unit_kernel(
    head_dim,
    x_ref,
    y_ref,
    n_ref,
    q_ref,
    k_ref,
    v_ref,
    proj_ref,
    out_ref,
    part_ref,
    dq_ref,
    dk_ref,
    dv_ref,
):
    inv_root = head_dim ** (-0.5)
    heads, _, inner = proj_ref.shape
    length = q_ref.shape[1]

    @pl.when(pl.program_id(0) < n_ref[0])
    def _():
        total = jnp.zeros((8, inner), jnp.float32)
        for h in range(heads):
            cols = slice(h * head_dim, (h + 1) * head_dim)
            q = q_ref[0, :, cols]
            k = k_ref[0, :, cols]
            v = v_ref[0, :, cols]
            proj = proj_ref[h]
            readout = out_ref[h : h + 1, :]
            scores = mm(q, k, NT) * inv_root
            lifted = jnp.exp(scores - jnp.max(scores, axis=-1, keepdims=True))
            weights = lifted * (1.0 / jnp.sum(lifted, axis=-1, keepdims=True))
            weights_bf = weights.astype(jnp.bfloat16)
            context = mm(weights_bf, v, NN).astype(jnp.bfloat16)
            hidden = mm(context, proj, NN)
            sig = 0.5 * jnp.tanh(0.5 * hidden) + 0.5
            silu = hidden * sig
            total += jnp.sum((silu * readout).reshape(length // 8, 8, inner), axis=0)
            dhidden = (readout * (sig + silu * (1.0 - sig))).astype(jnp.bfloat16)
            dcontext = mm(dhidden, proj, NT).astype(jnp.bfloat16)
            dv_ref[0, :, cols] = mm(weights_bf, dcontext, TN).astype(jnp.bfloat16)
            dweights = mm(dcontext, v, NT)
            inner_sum = jnp.sum(dweights * weights, axis=-1, keepdims=True)
            dscores = (weights * (dweights - inner_sum) * inv_root).astype(jnp.bfloat16)
            dq_ref[0, :, cols] = mm(dscores, k, NN).astype(jnp.bfloat16)
            dk_ref[0, :, cols] = mm(dscores, q, TN).astype(jnp.bfloat16)
        part_ref[0] = total


def run_units(unit_x, unit_y, count, q_all, k, v, head_proj, head_out):
    units = unit_x.shape[0]
    heads, head_dim, inner = head_proj.shape
    _, length, width = k.shape

    def out_map(u, x, y, n):
        return (jnp.minimum(u, n[0] - 1), 0, 0)

    rows = jax.ShapeDtypeStruct((units, length, width), jnp.bfloat16)
    row_spec = pl.BlockSpec((1, length, width), out_map)
    return pl.pallas_call(
        functools.partial(unit_kernel, head_dim),
        grid_spec=pltpu.PrefetchScalarGridSpec(
            num_scalar_prefetch=3,
            grid=(units,),
            in_specs=[
                pl.BlockSpec((1, length, width), lambda u, x, y, n: (x[u], 0, 0)),
                pl.BlockSpec((1, length, width), lambda u, x, y, n: (y[u], 0, 0)),
                pl.BlockSpec((1, length, width), lambda u, x, y, n: (y[u], 0, 0)),
                pl.BlockSpec((heads, head_dim, inner), lambda u, x, y, n: (0, 0, 0)),
                pl.BlockSpec((heads, inner), lambda u, x, y, n: (0, 0)),
            ],
            out_specs=[pl.BlockSpec((1, 8, inner), out_map), row_spec, row_spec, row_spec],
        ),
        out_shape=[jax.ShapeDtypeStruct((units, 8, inner), jnp.float32), rows, rows, rows],
        compiler_params=pltpu.CompilerParams(
            dimension_semantics=("arbitrary",), vmem_limit_bytes=32 * 1024 * 1024
        ),
        cost_estimate=pl.CostEstimate(
            flops=20 * units * heads * length * length * head_dim,
            bytes_accessed=12 * units * length * width,
            transcendentals=units * heads * length * (length + inner),
        ),
    )(unit_x, unit_y, count, q_all, k, v, head_proj, head_out)


def sum_kernel(
    x_ref, y_ref, n_ref, g_ref, dq_ref, dk_ref, dv_ref, oq_ref, ok_ref, ov_ref, sq, sk, sv
):
    sq[...] = jnp.zeros_like(sq)
    sk[...] = jnp.zeros_like(sk)
    sv[...] = jnp.zeros_like(sv)

    def step(u, carry):
        x = x_ref[u]
        y = y_ref[u]
        g = g_ref[u]
        sq[x] += g * dq_ref[u].astype(jnp.float32)
        sk[y] += g * dk_ref[u].astype(jnp.float32)
        sv[y] += g * dv_ref[u].astype(jnp.float32)
        return carry

    lax.fori_loop(0, n_ref[0], step, 0)
    oq_ref[...] = sq[...].astype(jnp.bfloat16)
    ok_ref[...] = sk[...].astype(jnp.bfloat16)
    ov_ref[...] = sv[...].astype(jnp.bfloat16)


def run_sums(unit_x, unit_y, count, scale, dq, dk, dv, mols_all, mols_here):
    units, length, width = dq.shape
    in_spec = pl.BlockSpec((units, row_block, width), lambda i, x, y, n, g: (0, i, 0))
    all_spec = pl.BlockSpec((mols_all, row_block, width), lambda i, x, y, n, g: (0, i, 0))
    here_spec = pl.BlockSpec((mols_here, row_block, width), lambda i, x, y, n, g: (0, i, 0))
    here = jax.ShapeDtypeStruct((mols_here, length, width), jnp.bfloat16)
    return pl.pallas_call(
        sum_kernel,
        grid_spec=pltpu.PrefetchScalarGridSpec(
            num_scalar_prefetch=4,
            grid=(length // row_block,),
            in_specs=[in_spec] * 3,
            out_specs=[all_spec, here_spec, here_spec],
            scratch_shapes=[
                pltpu.VMEM((mols_all, row_block, width), jnp.float32),
                pltpu.VMEM((mols_here, row_block, width), jnp.float32),
                pltpu.VMEM((mols_here, row_block, width), jnp.float32),
            ],
        ),
        out_shape=[jax.ShapeDtypeStruct((mols_all, length, width), jnp.bfloat16), here, here],
        compiler_params=pltpu.CompilerParams(
            dimension_semantics=("arbitrary",), vmem_limit_bytes=40 * 1024 * 1024
        ),
        cost_estimate=pl.CostEstimate(
            flops=6 * units * length * width,
            bytes_accessed=2 * (3 * units + mols_all + 2 * mols_here) * length * width,
            transcendentals=0,
        ),
    )(unit_x, unit_y, count, scale, dq, dk, dv)


def local(mol_qkv, pair_list, head_proj, head_out, labels):
    groups = lax.axis_size("group")
    device = lax.axis_index("group")
    mols_here, length, _, row_width = mol_qkv.shape
    heads_here, head_dim, _ = head_proj.shape
    total_pairs = pair_list.shape[0]
    per_owner = total_pairs // groups
    mols_all = mols_here * groups
    held = groups * (2 * per_owner // groups)
    width = row_width // chunks
    heads_each = heads_here // chunks

    pairs = jnp.arange(total_pairs, dtype=jnp.int32)
    owner = pairs // per_owner
    first_all = owner * mols_here + pair_list[:, 0]
    second_all = pair_list[:, 1] * mols_here + pair_list[:, 2]
    own_pair = device * per_owner + jnp.arange(per_owner, dtype=jnp.int32)
    own_x = lax.dynamic_slice_in_dim(second_all, device * per_owner, per_owner)
    own_y = lax.dynamic_slice_in_dim(pair_list[:, 0], device * per_owner, per_owner)
    here = pair_list[:, 1] == device
    rank = jnp.cumsum(here.astype(jnp.int32)) - 1
    slots = jnp.arange(held, dtype=jnp.int32)
    pick = (here[None, :] & (rank[None, :] == slots[:, None])).astype(jnp.int32)
    held_x = jnp.sum(pick * first_all[None, :], axis=1)
    held_y = jnp.sum(pick * pair_list[:, 2][None, :], axis=1)
    held_pair = jnp.sum(pick * pairs[None, :], axis=1)
    unit_x = jnp.concatenate([own_x, held_x]).astype(jnp.int32)
    unit_y = jnp.concatenate([own_y, held_y]).astype(jnp.int32)
    unit_pair = jnp.concatenate([own_pair, held_pair])
    active = per_owner + jnp.sum(here.astype(jnp.int32))
    count = active.reshape(1).astype(jnp.int32)
    valid = jnp.arange(per_owner + held, dtype=jnp.int32) < active
    at_pair = (unit_pair[:, None] == pairs[None, :]) & valid[:, None]

    results = []
    part = 0.0
    for c in range(chunks):
        cols = slice(c * width, (c + 1) * width)
        hs = slice(c * heads_each, (c + 1) * heads_each)
        q_all = lax.all_gather(mol_qkv[:, :, 0, cols], "group", axis=0, tiled=True)
        k = mol_qkv[:, :, 1, cols]
        v = mol_qkv[:, :, 2, cols]
        sums, dq, dk, dv = run_units(
            unit_x, unit_y, count, q_all, k, v, head_proj[hs], head_out[hs]
        )
        part = part + jnp.sum(sums, axis=(1, 2))
        results.append((dq, dk, dv))

    terms = jnp.sum(jnp.where(at_pair, part[:, None], 0.0), axis=0) / length
    first_copy = (lax.axis_index("fsdp") == 0).astype(jnp.float32)
    spread = lax.dynamic_update_slice_in_dim(
        jnp.zeros((total_pairs,), jnp.float32),
        labels.astype(jnp.float32) * first_copy,
        device * per_owner,
        0,
    )
    both = lax.psum(jnp.stack([terms, spread]), ("group", "fsdp"))
    logits, targets = both[0], both[1]
    mean_loss = jnp.sum(jax.nn.softplus(logits) - targets * logits) / total_pairs
    grad_out = (jax.nn.sigmoid(logits) - targets) * loss_scale
    scale = jnp.sum(jnp.where(at_pair, grad_out[None, :], 0.0), axis=1) / length

    dqs, dks, dvs = [], [], []
    for dq, dk, dv in results:
        sq, sk, sv = run_sums(
            unit_x, unit_y, count, scale, dq, dk, dv, mols_all, mols_here
        )
        dqs.append(lax.psum_scatter(sq, "group", scatter_dimension=0, tiled=True))
        dks.append(sk)
        dvs.append(sv)
    mol_grad = jnp.stack(
        [jnp.concatenate(d, axis=-1) for d in (dqs, dks, dvs)], axis=2
    )
    own_logits = lax.dynamic_slice_in_dim(logits, device * per_owner, per_owner)
    return (mol_grad, own_logits, mean_loss)


def solution(mesh):
    placed = (
        P("group", None, None, "fsdp"),
        P(),
        P("fsdp", None, None),
        P("fsdp", None),
        P("group"),
    )
    return jax.shard_map(
        local,
        mesh=mesh,
        in_specs=placed,
        out_specs=(P("group", None, None, "fsdp"), P("group"), P()),
        check_vma=False,
    )
```

time: 1080 us -> 770 us (0.71)
  matrix products: 250 us -> 0 us
  Pallas kernels: 0 us -> 226 us
  blocking collectives: 288 us -> 76 us
  local copies, waits for them, and re-layouts: 230 us -> 37.4 us
  waiting for transfers between devices: 228 us -> 407 us
  other arithmetic: 61.2 us -> 11.1 us
  between operations: 2.97 us -> 16.4 us
  starting transfers between devices: 12.7 us -> 0.16 us
    reduce_scatter x0 -> x2, waiting for transfers between devices: none -> 274 us  [local(): dqs.append(lax.psum_scatter(sq, 'group', scatter_dimension=0, tiled=True))]
    dot_general x15 -> x0, matrix products: 231 us -> none  [the longest x2 36.2 us: backward(): jnp.einsum('phlm,plhd->pmhd', dscores, query_rows, preferred_element_type...]
    all_to_all x2 -> x0, waiting for transfers between devices: 228 us -> none  [the longest x1 228 us: local(): lax.all_to_all(outgoing, 'group', split_axis=0, concat_axis=0, tiled=True)]
    pallas_call x0 -> x4, Pallas kernels: none -> 226 us  [the longest x2 200 us: run_units(): pl.pallas_call(functools.partial(unit_kernel, head_dim), grid_spec=pltpu....]
    psum x2 -> x1, blocking collectives: 288 us -> 76 us  [local(): both = lax.psum(jnp.stack([terms, spread]), ('group', 'fsdp'))]
    all_gather x0 -> x2, waiting for transfers between devices: none -> 132 us  [local(): q_all = lax.all_gather(mol_qkv[:, :, 0, cols], 'group', axis=0, tiled=True)]
    reshape x5 -> x0, local copies, waits for them, and re-layouts: 71.9 us -> none  [the longest x2 42.3 us: local(): outgoing_grad.astype(jnp.bfloat16).reshape(slots_all, length, 3, row_width)]
    another operation x2 -> x0, local copies, waits for them, and re-layouts: 49.5 us -> none  [the longest x1 24.8 us: local(): grad_first = jnp.stack([dq_a, dk_a, dv_a], axis=2).reshape(per_owner, -1)]
  transfers between devices with their start and end apart: 2 -> 4, of which waited for: 1 -> 4; matrix products, arithmetic and copies ran while one was open for 15% -> 1% of each run, Pallas kernels for 0% -> 15%
where the time goes in v1:
time: 770 us; the launch traced here: 773 us
  waiting for transfers between devices  407 us (53%)
  Pallas kernels  226 us (29%)
  blocking collectives  76 us (10%)
  local copies, waits for them, and re-layouts  37.4 us (5%)
  between operations  16.4 us (2%)
  other arithmetic  11.1 us (1%)
    reduce_scatter x2, waiting for transfers between devices, local(): dqs.append(lax.psum_scatter(sq, 'group', scatter_dimension=0, tiled=True))  274 us
    pallas_call x2, Pallas kernels, run_units(): pl.pallas_call(functools.partial(unit_kernel, head_dim), grid_spec=pltpu....  200 us
    all_gather x2, waiting for transfers between devices, local(): q_all = lax.all_gather(mol_qkv[:, :, 0, cols], 'group', axis=0, tiled=True)  132 us
    psum x1, blocking collectives, local(): both = lax.psum(jnp.stack([terms, spread]), ('group', 'fsdp'))  76 us
    unnamed x43, local copies, waits for them, and re-layouts  29.7 us
    pallas_call x2, Pallas kernels, run_sums(): pl.pallas_call(sum_kernel, grid_spec=pltpu.PrefetchScalarGridSpec(num_sca...  25.1 us
  transfers between devices with their start and end apart: 4, of which 4 were waited for; matrix products, arithmetic and copies ran while one was open for 1% of the time, Pallas kernels for 15%

profile of v1, /device:TPU:8, one launch (start us, length us, event | category | flops | bytes accessed | tf_op | source)
XLA Modules:
  0.0 773.4 jit_solution(17393435000244567871)
XLA Ops:
  7.2 4.8 slice_bitcast_fusion
  16.9 1.8 fusion.10
  18.7 117.3 %all-gather.7.cloned.1.call-done = bf16[64,128,1,512]{3,1,2,0:T(8,128)(2,1)} async-done(((bf16[8,128,1,512]{3,1,2,0:T(8,128)(2,1)}), bf16[64,128,1,512]{3,1,2,0:T(8,128)(2,1)}) %all-gather.7.cloned.1.call-update) | async-done | bytes 8388624 | tf_op jit(solution)/shard_map/all_gather | solution.py:200
  136.0 1.2 copy-done.8
  138.2 100.2 %shard_map.77 = (f32[48,8,256]{2,1,0:T(8,128)S(1)}, bf16[48,128,512]{2,1,0:T(8,128)(2,1)S(1)}, bf16[48,128,512]{2,1,0:T(8,128)(2,1)S(1)}, bf16[48,128,512]{2,1,0:T(8,128)(2,1)S(1)}) custom-call(s32[48]{0:T(128)S(1)} %get-tuple-element.66.x_ref, s32[48]{0:T(128)S(1)} %get-tuple-element.67.y_ref, s32[1]{0:T(128)} %bitcast.5.n_ref, ...), custom_call_target="tpu_custom_call" | custom-call | flops 8053063680 | bytes 37748736 | tf_op jit(solution)/shard_map/pallas_call | solution.py:82
  238.4 2.7 copy-done.4
  241.1 2.7 copy-done.6
  243.8 2.6 copy-done.7
  246.8 14.6 %all-gather.5.cloned.1.call-done = bf16[64,128,1,512]{3,1,2,0:T(8,128)(2,1)} async-done(((bf16[8,128,1,512]{3,1,2,0:T(8,128)(2,1)}), bf16[64,128,1,512]{3,1,2,0:T(8,128)(2,1)}) %all-gather.5.cloned.1.call-update) | async-done | bytes 8388624 | tf_op jit(solution)/shard_map/all_gather | solution.py:200
  262.4 100.2 %shard_map.76 = (f32[48,8,256]{2,1,0:T(8,128)S(1)}, bf16[48,128,512]{2,1,0:T(8,128)(2,1)S(1)}, bf16[48,128,512]{2,1,0:T(8,128)(2,1)S(1)}, bf16[48,128,512]{2,1,0:T(8,128)(2,1)S(1)}) custom-call(s32[48]{0:T(128)S(1)} %get-tuple-element.66.x_ref, s32[48]{0:T(128)S(1)} %get-tuple-element.67.y_ref, s32[1]{0:T(128)} %bitcast.5.n_ref, ...), custom_call_target="tpu_custom_call" | custom-call | flops 8053063680 | bytes 37748736 | tf_op jit(solution)/shard_map/pallas_call | solution.py:82
  362.6 2.6 copy-done
  365.2 2.6 copy-done.2
  367.8 2.6 copy-done.3
  371.0 76.0 %psum.7 = f32[2,128]{1,0:T(2,128)S(1)} all-reduce(f32[2,128]{1,0:T(2,128)S(1)} %pad_maximum_fusion.1), channel_id=1, replica_groups=mesh['group'=8,'fsdp'=4] {'group','fsdp'}, use_global_device_ids=true, to_apply=%region_8.9 | all-reduce | flops 256 | bytes 2048 | tf_op jit(solution)/shard_map/psum | solution.py:217
  447.3 2.8 copy-done.5
  450.1 12.4 %shard_map.79 = (bf16[64,128,512]{2,1,0:T(8,128)(2,1)}, bf16[8,128,512]{2,1,0:T(8,128)(2,1)S(1)}, bf16[8,128,512]{2,1,0:T(8,128)(2,1)S(1)}) custom-call(s32[48]{0:T(128)S(1)} %get-tuple-element.66.x_ref, s32[48]{0:T(128)S(1)} %get-tuple-element.67.y_ref, s32[1]{0:T(128)} %bitcast.5.n_ref, f32[48]{0:T(128)S(1)} %broadcast_multiply_fusion.g_ref, ...), custom_call_target="tpu_custom_call" | custom-call | flops 18874368 | bytes 29360128 | tf_op jit(solution)/shard_map/pallas_call | solution.py:136
  462.5 2.8 copy-done.1
  465.3 12.7 %shard_map.78 = (bf16[64,128,512]{2,1,0:T(8,128)(2,1)}, bf16[8,128,512]{2,1,0:T(8,128)(2,1)S(1)}, bf16[8,128,512]{2,1,0:T(8,128)(2,1)S(1)}) custom-call(s32[48]{0:T(128)S(1)} %get-tuple-element.66.x_ref, s32[48]{0:T(128)S(1)} %get-tuple-element.67.y_ref, s32[1]{0:T(128)} %bitcast.5.n_ref, f32[48]{0:T(128)S(1)} %broadcast_multiply_fusion.g_ref, ...), custom_call_target="tpu_custom_call" | custom-call | flops 18874368 | bytes 29360128 | tf_op jit(solution)/shard_map/pallas_call | solution.py:136
  480.9 2.8 maximum_bitcast_fusion.1
  483.7 1.6 maximum_bitcast_fusion.2
  485.3 124.0 %reduce-scatter.5.cloned.1.call-done = bf16[8,128,512]{2,1,0:T(8,128)(2,1)} async-done(((bf16[64,128,512]{2,1,0:T(8,128)(2,1)}), bf16[8,128,512]{2,1,0:T(8,128)(2,1)}) %reduce-scatter.5.cloned.1.call-update) | async-done | bytes 1048592 | tf_op jit(solution)/shard_map/reduce_scatter | solution.py:228
  609.3 150.1 %reduce-scatter.3.cloned.1.call-done = bf16[8,128,512]{2,1,0:T(8,128)(2,1)} async-done(((bf16[64,128,512]{2,1,0:T(8,128)(2,1)}), bf16[8,128,512]{2,1,0:T(8,128)(2,1)}) %reduce-scatter.3.cloned.1.call-update) | async-done | bytes 1048592 | tf_op jit(solution)/shard_map/reduce_scatter | solution.py:228
  759.4 1.9 maximum_bitcast_fusion
  762.3 3.4 copy.35
  (70 shorter events, 10.5 us)
Async XLA Ops:
  7.2 5.7 copy-start.15
  7.2 7.4 copy-start.20
  7.2 9.7 %copy-start.14 = (f32[8,256]{1,0:T(8,128)S(1)}, f32[8,256]{1,0:T(8,128)}, u32[]{:S(2)}) copy-start(f32[8,256]{1,0:T(8,128)} %param.8) | copy-start | bytes 24580
  7.2 128.8 %all-gather.7.cloned.1.call-start = ((), (), s32[]{:S(2)}) async-start(), calls=%async_computation.5 | async-start | bytes 9437184 | tf_op jit(solution)/shard_map/all_gather | solution.py:200
  12.1 249.3 %all-gather.5.cloned.1.call-start = ((), (), s32[]{:S(2)}) async-start(), calls=%async_computation.4 | async-start | bytes 9437184 | tf_op jit(solution)/shard_map/all_gather | solution.py:200
  12.8 596.5 %reduce-scatter.5.cloned.1.call-start = ((), (), s32[]{:S(2)}) async-start(), calls=%async_computation.3 | async-start | bytes 9437184 | tf_op jit(solution)/shard_map/reduce_scatter | solution.py:228
  136.0 1.2 copy-start.8
  137.2 0.9 copy-start.11
  238.4 2.7 copy-start.4
  241.1 2.7 copy-start.6
  243.8 2.6 copy-start.7
  261.4 0.9 copy-start.10
  262.4 108.5 %copy-start.16 = (pred[48]{0:T(512)(128)(4,1)S(1)}, pred[48]{0:T(512)(128)(4,1)}, u32[]{:S(2)}) copy-start(pred[48]{0:T(512)(128)(4,1)} %iota_compare_fusion.2) | copy-start | bytes 148
  262.4 108.5 %copy-start.17 = (s32[48]{0:T(128)S(1)}, s32[48]{0:T(128)}, u32[]{:S(2)}) copy-start(s32[48]{0:T(128)} %pad_add_fusion.2) | copy-start | bytes 580
  262.4 108.6 %copy-start.19 = (f32[1,128]{1,0:T(1,128)S(1)}, f32[1,128]{1,0:T(1,128)}, u32[]{:S(2)}) copy-start(f32[1,128]{1,0:T(1,128)} %copy-done.18) | copy-start | bytes 1540
  362.6 2.6 copy-start
  365.2 2.6 copy-start.2
  367.8 2.6 copy-start.3
  447.3 2.8 copy-start.5
  462.5 296.9 %reduce-scatter.3.cloned.1.call-start = ((), (), s32[]{:S(2)}) async-start(), calls=%async_computation.2 | async-start | bytes 9437184 | tf_op jit(solution)/shard_map/reduce_scatter | solution.py:228
  462.5 2.8 copy-start.1
  478.0 1.0 copy-start.9
  485.3 276.0 %copy-start.12 = (bf16[8,128,1,1024]{3,1,0,2:T(8,128)(2,1)S(1)}, bf16[8,128,1,1024]{3,1,0,2:T(8,128)(2,1)}, u32[]{:S(2)}) copy-start(bf16[8,128,1,1024]{3,1,0,2:T(8,128)(2,1)} %maximum_bitcast_fusion.1) | copy-start | bytes 6291460
  759.4 2.2 copy-start.13
  (1 other events, 0.5 us)
Sparse Core Ops, SparseCore 0:
  12.2 123.7 all-gather.6
  138.1 123.2 all-gather.4
  462.6 146.6 reduce-scatter.4
  612.8 146.5 reduce-scatter.2

commit v2 on v1

--- a/solution.py
+++ b/solution.py
@@ -8,7 +8,7 @@
 from jax.sharding import PartitionSpec as P
 
 loss_scale = 8192.0
-chunks = 2
+most_chunks = 4
 row_block = 16
 
 NN = (((1,), (0,)), ((), ()))
@@ -95,7 +95,7 @@
         ),
         out_shape=[jax.ShapeDtypeStruct((units, 8, inner), jnp.float32), rows, rows, rows],
         compiler_params=pltpu.CompilerParams(
-            dimension_semantics=("arbitrary",), vmem_limit_bytes=32 * 1024 * 1024
+            dimension_semantics=("arbitrary",), vmem_limit_bytes=60 * 1024 * 1024
         ),
         cost_estimate=pl.CostEstimate(
             flops=20 * units * heads * length * length * head_dim,
@@ -148,7 +148,7 @@
         ),
         out_shape=[jax.ShapeDtypeStruct((mols_all, length, width), jnp.bfloat16), here, here],
         compiler_params=pltpu.CompilerParams(
-            dimension_semantics=("arbitrary",), vmem_limit_bytes=40 * 1024 * 1024
+            dimension_semantics=("arbitrary",), vmem_limit_bytes=60 * 1024 * 1024
         ),
         cost_estimate=pl.CostEstimate(
             flops=6 * units * length * width,
@@ -167,6 +167,7 @@
     per_owner = total_pairs // groups
     mols_all = mols_here * groups
     held = groups * (2 * per_owner // groups)
+    chunks = min(most_chunks, heads_here)
     width = row_width // chunks
     heads_each = heads_here // chunks
 
@@ -214,7 +215,8 @@
         device * per_owner,
         0,
     )
-    both = lax.psum(jnp.stack([terms, spread]), ("group", "fsdp"))
+    shares = lax.all_gather(jnp.stack([terms, spread]), ("group", "fsdp"), axis=0)
+    both = jnp.sum(shares, axis=0)
     logits, targets = both[0], both[1]
     mean_loss = jnp.sum(jax.nn.softplus(logits) - targets * logits) / total_pairs
     grad_out = (jax.nn.sigmoid(logits) - targets) * loss_scale

time: 770 us -> 803 us (1.043)
  Pallas kernels: 226 us -> 305 us
  blocking collectives: 76 us -> 33.2 us
  local copies, waits for them, and re-layouts: 37.4 us -> 11.8 us
  waiting for transfers between devices: 407 us -> 417 us
    psum x1 -> x0, blocking collectives: 76 us -> none  [local(): both = lax.psum(jnp.stack([terms, spread]), ('group', 'fsdp'))]
    pallas_call x2 -> x4, Pallas kernels: 200 us -> 264 us  [run_units(): pl.pallas_call(functools.partial(unit_kernel, head_dim), grid_spec=pltpu....]
    reduce_scatter x2 -> x4, waiting for transfers between devices: 274 us -> 328 us  [local(): dqs.append(lax.psum_scatter(sq, 'group', scatter_dimension=0, tiled=True))]
    all_gather x2 -> x4, waiting for transfers between devices: 132 us -> 86.5 us  [local(): q_all = lax.all_gather(mol_qkv[:, :, 0, cols], 'group', axis=0, tiled=True)]
    all_gather x0 -> x1, blocking collectives: none -> 33.2 us  [local(): lax.all_gather(jnp.stack([terms, spread]), ('group', 'fsdp'), axis=0)]
    unnamed x43 -> x15, local copies, waits for them, and re-layouts: 29.7 us -> 3.71 us
    pallas_call x2 -> x4, Pallas kernels: 25.1 us -> 41.1 us  [run_sums(): pl.pallas_call(sum_kernel, grid_spec=pltpu.PrefetchScalarGridSpec(num_sca...]
  transfers between devices with their start and end apart: 4 -> 8, of which waited for: 4 -> 8; matrix products, arithmetic and copies ran while one was open for 1% -> 2% of each run, Pallas kernels for 15% -> 29%
where the time goes in v2:
time: 803 us; the launch traced here: 800 us
  waiting for transfers between devices  417 us (52%)
  Pallas kernels  305 us (38%)
  blocking collectives  33.2 us (4%)
  between operations  16.7 us (2%)
  other arithmetic  16.3 us (2%)
  local copies, waits for them, and re-layouts  11.8 us (1%)
    reduce_scatter x4, waiting for transfers between devices, local(): dqs.append(lax.psum_scatter(sq, 'group', scatter_dimension=0, tiled=True))  328 us
    pallas_call x4, Pallas kernels, run_units(): pl.pallas_call(functools.partial(unit_kernel, head_dim), grid_spec=pltpu....  264 us
    all_gather x4, waiting for transfers between devices, local(): q_all = lax.all_gather(mol_qkv[:, :, 0, cols], 'group', axis=0, tiled=True)  86.5 us
    pallas_call x4, Pallas kernels, run_sums(): pl.pallas_call(sum_kernel, grid_spec=pltpu.PrefetchScalarGridSpec(num_sca...  41.1 us
    all_gather x1, blocking collectives, local(): lax.all_gather(jnp.stack([terms, spread]), ('group', 'fsdp'), axis=0)  33.2 us
  transfers between devices with their start and end apart: 8, of which 8 were waited for; matrix products, arithmetic and copies ran while one was open for 2% of the time, Pallas kernels for 29%

profile of v2, /device:TPU:8, one launch (start us, length us, event | category | flops | bytes accessed | tf_op | source)
XLA Modules:
  0.0 799.8 jit_solution(885833680419736787)
XLA Ops:
  7.3 5.6 slice_bitcast_fusion.4
  19.4 67.3 %all-gather.15.cloned.1.call-done = bf16[64,128,1,256]{3,1,2,0:T(8,128)(2,1)} async-done(((bf16[8,128,1,256]{3,1,2,0:T(8,128)(2,1)}), bf16[64,128,1,256]{3,1,2,0:T(8,128)(2,1)}) %all-gather.15.cloned.1.call-update) | async-done | bytes 4194320 | tf_op jit(solution)/shard_map/all_gather | solution.py:201
  86.7 65.9 %shard_map.78 = (f32[48,8,256]{2,1,0:T(8,128)}, bf16[48,128,256]{2,1,0:T(8,128)(2,1)}, bf16[48,128,256]{2,1,0:T(8,128)(2,1)}, bf16[48,128,256]{2,1,0:T(8,128)(2,1)}) custom-call(s32[48]{0:T(128)} %get-tuple-element.104.x_ref, s32[48]{0:T(128)} %get-tuple-element.105.y_ref, s32[1]{0:T(128)} %bitcast.5.n_ref, bf16[64,128,256]{2,1,0:T(8,128)(2,1)} %bitcast.93, ...), custom_call_target="tpu_custom_call" | custom-call | flops 4026531840 | bytes 18874368 | tf_op jit(solution)/shard_map/pallas_call | solution.py:82
  152.6 1.4 reduce_sum.114
  154.1 6.7 all-gather.13.cloned.1.call-done
  160.8 66.0 %shard_map.77 = (f32[48,8,256]{2,1,0:T(8,128)}, bf16[48,128,256]{2,1,0:T(8,128)(2,1)}, bf16[48,128,256]{2,1,0:T(8,128)(2,1)}, bf16[48,128,256]{2,1,0:T(8,128)(2,1)}) custom-call(s32[48]{0:T(128)} %get-tuple-element.104.x_ref, s32[48]{0:T(128)} %get-tuple-element.105.y_ref, s32[1]{0:T(128)} %bitcast.5.n_ref, bf16[64,128,256]{2,1,0:T(8,128)(2,1)} %bitcast.92, ...), custom_call_target="tpu_custom_call" | custom-call | flops 4026531840 | bytes 18874368 | tf_op jit(solution)/shard_map/pallas_call | solution.py:82
  228.2 6.1 all-gather.11.cloned.1.call-done
  234.3 65.9 %shard_map.76 = (f32[48,8,256]{2,1,0:T(8,128)}, bf16[48,128,256]{2,1,0:T(8,128)(2,1)}, bf16[48,128,256]{2,1,0:T(8,128)(2,1)}, bf16[48,128,256]{2,1,0:T(8,128)(2,1)}) custom-call(s32[48]{0:T(128)} %get-tuple-element.104.x_ref, s32[48]{0:T(128)} %get-tuple-element.105.y_ref, s32[1]{0:T(128)} %bitcast.5.n_ref, bf16[64,128,256]{2,1,0:T(8,128)(2,1)} %bitcast.91, ...), custom_call_target="tpu_custom_call" | custom-call | flops 4026531840 | bytes 18874368 | tf_op jit(solution)/shard_map/pallas_call | solution.py:82
  301.7 6.4 all-gather.17.cloned.1.call-done
  308.0 65.9 %shard_map.79 = (f32[48,8,256]{2,1,0:T(8,128)}, bf16[48,128,256]{2,1,0:T(8,128)(2,1)}, bf16[48,128,256]{2,1,0:T(8,128)(2,1)}, bf16[48,128,256]{2,1,0:T(8,128)(2,1)}) custom-call(s32[48]{0:T(128)} %get-tuple-element.104.x_ref, s32[48]{0:T(128)} %get-tuple-element.105.y_ref, s32[1]{0:T(128)} %bitcast.5.n_ref, bf16[64,128,256]{2,1,0:T(8,128)(2,1)} %bitcast.90, ...), custom_call_target="tpu_custom_call" | custom-call | flops 4026531840 | bytes 18874368 | tf_op jit(solution)/shard_map/pallas_call | solution.py:82
  373.9 1.4 reduce_sum.115
  375.5 33.2 %all-gather.5 = f32[32,2,128]{2,1,0:T(2,128)S(1)} all-gather(f32[1,2,128]{2,1,0:T(2,128)S(1)} %maximum_bitcast_fusion.3), channel_id=6, replica_groups=mesh['group'=8,'fsdp'=4] {'group','fsdp'}, dimensions={0}, use_global_device_ids=true | all-gather | bytes 33792 | tf_op jit(solution)/shard_map/all_gather | solution.py:218
  409.6 10.1 %shard_map.83 = (bf16[64,128,256]{2,1,0:T(8,128)(2,1)}, bf16[8,128,256]{2,1,0:T(8,128)(2,1)}, bf16[8,128,256]{2,1,0:T(8,128)(2,1)}) custom-call(s32[48]{0:T(128)} %get-tuple-element.104.x_ref, s32[48]{0:T(128)} %get-tuple-element.105.y_ref, s32[1]{0:T(128)} %bitcast.5.n_ref, f32[48]{0:T(128)} %broadcast_multiply_fusion.g_ref, ...), custom_call_target="tpu_custom_call" | custom-call | flops 9437184 | bytes 14680064 | tf_op jit(solution)/shard_map/pallas_call | solution.py:136
  419.7 10.2 %shard_map.82 = (bf16[64,128,256]{2,1,0:T(8,128)(2,1)}, bf16[8,128,256]{2,1,0:T(8,128)(2,1)}, bf16[8,128,256]{2,1,0:T(8,128)(2,1)}) custom-call(s32[48]{0:T(128)} %get-tuple-element.104.x_ref, s32[48]{0:T(128)} %get-tuple-element.105.y_ref, s32[1]{0:T(128)} %bitcast.5.n_ref, f32[48]{0:T(128)} %broadcast_multiply_fusion.g_ref, ...), custom_call_target="tpu_custom_call" | custom-call | flops 9437184 | bytes 14680064 | tf_op jit(solution)/shard_map/pallas_call | solution.py:136
  430.0 10.2 %shard_map.81 = (bf16[64,128,256]{2,1,0:T(8,128)(2,1)}, bf16[8,128,256]{2,1,0:T(8,128)(2,1)}, bf16[8,128,256]{2,1,0:T(8,128)(2,1)}) custom-call(s32[48]{0:T(128)} %get-tuple-element.104.x_ref, s32[48]{0:T(128)} %get-tuple-element.105.y_ref, s32[1]{0:T(128)} %bitcast.5.n_ref, f32[48]{0:T(128)} %broadcast_multiply_fusion.g_ref, ...), custom_call_target="tpu_custom_call" | custom-call | flops 9437184 | bytes 14680064 | tf_op jit(solution)/shard_map/pallas_call | solution.py:136
  440.3 10.6 %shard_map.80 = (bf16[64,128,256]{2,1,0:T(8,128)(2,1)}, bf16[8,128,256]{2,1,0:T(8,128)(2,1)}, bf16[8,128,256]{2,1,0:T(8,128)(2,1)}) custom-call(s32[48]{0:T(128)} %get-tuple-element.104.x_ref, s32[48]{0:T(128)} %get-tuple-element.105.y_ref, s32[1]{0:T(128)} %bitcast.5.n_ref, f32[48]{0:T(128)} %broadcast_multiply_fusion.g_ref, ...), custom_call_target="tpu_custom_call" | custom-call | flops 9437184 | bytes 14680064 | tf_op jit(solution)/shard_map/pallas_call | solution.py:136
  452.8 1.6 maximum_bitcast_fusion.1
  454.4 3.0 maximum_bitcast_fusion.2
  457.4 53.4 %reduce-scatter.11.cloned.1.call-done = bf16[8,128,256]{2,1,0:T(8,128)(2,1)} async-done(((bf16[64,128,256]{2,1,0:T(8,128)(2,1)}), bf16[8,128,256]{2,1,0:T(8,128)(2,1)}) %reduce-scatter.11.cloned.1.call-update) | async-done | bytes 524304 | tf_op jit(solution)/shard_map/reduce_scatter | solution.py:230
  510.8 91.5 %reduce-scatter.9.cloned.1.call-done = bf16[8,128,256]{2,1,0:T(8,128)(2,1)} async-done(((bf16[64,128,256]{2,1,0:T(8,128)(2,1)}), bf16[8,128,256]{2,1,0:T(8,128)(2,1)}) %reduce-scatter.9.cloned.1.call-update) | async-done | bytes 524304 | tf_op jit(solution)/shard_map/reduce_scatter | solution.py:230
  602.3 91.6 %reduce-scatter.7.cloned.1.call-done = bf16[8,128,256]{2,1,0:T(8,128)(2,1)} async-done(((bf16[64,128,256]{2,1,0:T(8,128)(2,1)}), bf16[8,128,256]{2,1,0:T(8,128)(2,1)}) %reduce-scatter.7.cloned.1.call-update) | async-done | bytes 524304 | tf_op jit(solution)/shard_map/reduce_scatter | solution.py:230
  693.9 91.6 %reduce-scatter.5.cloned.1.call-done = bf16[8,128,256]{2,1,0:T(8,128)(2,1)} async-done(((bf16[64,128,256]{2,1,0:T(8,128)(2,1)}), bf16[8,128,256]{2,1,0:T(8,128)(2,1)}) %reduce-scatter.5.cloned.1.call-update) | async-done | bytes 524304 | tf_op jit(solution)/shard_map/reduce_scatter | solution.py:230
  785.5 1.9 maximum_bitcast_fusion
  788.4 3.4 copy.55
  (61 shorter events, 12.0 us)
Async XLA Ops:
  7.2 7.9 copy-start.5
  7.2 9.5 %copy-start.6 = (s32[16]{0:T(128)S(1)}, s32[16]{0:T(128)}, u32[]{:S(2)}) copy-start(s32[16]{0:T(128)} %param.9) | copy-start | bytes 196
  7.2 10.8 %copy-start.4 = (f32[8,256]{1,0:T(8,128)S(1)}, f32[8,256]{1,0:T(8,128)}, u32[]{:S(2)}) copy-start(f32[8,256]{1,0:T(8,128)} %param.8) | copy-start | bytes 24580
  7.2 11.4 %copy-start.1 = (bf16[8,128,256]{2,1,0:T(8,128)(2,1)S(1)}, bf16[8,128,256]{2,1,0:T(8,128)(2,1)}, u32[]{:S(2)}) copy-start(bf16[8,128,256]{2,1,0:T(8,128)(2,1)} %param.7) | copy-start | bytes 1572868
  7.2 79.5 %all-gather.15.cloned.1.call-start = ((), (), s32[]{:S(2)}) async-start(), calls=%async_computation.10 | async-start | bytes 4718592 | tf_op jit(solution)/shard_map/all_gather | solution.py:201
  12.9 147.9 %all-gather.13.cloned.1.call-start = ((), (), s32[]{:S(2)}) async-start(), calls=%async_computation.9 | async-start | bytes 4718592 | tf_op jit(solution)/shard_map/all_gather | solution.py:201
  13.7 220.6 %all-gather.11.cloned.1.call-start = ((), (), s32[]{:S(2)}) async-start(), calls=%async_computation.8 | async-start | bytes 4718592 | tf_op jit(solution)/shard_map/all_gather | solution.py:201
  14.4 293.6 %all-gather.17.cloned.1.call-start = ((), (), s32[]{:S(2)}) async-start(), calls=%async_computation.11 | async-start | bytes 4718592 | tf_op jit(solution)/shard_map/all_gather | solution.py:201
  15.0 495.9 %reduce-scatter.11.cloned.1.call-start = ((), (), s32[]{:S(2)}) async-start(), calls=%async_computation.7 | async-start | bytes 4718592 | tf_op jit(solution)/shard_map/reduce_scatter | solution.py:230
  419.7 182.6 %reduce-scatter.9.cloned.1.call-start = ((), (), s32[]{:S(2)}) async-start(), calls=%async_computation.6 | async-start | bytes 4718592 | tf_op jit(solution)/shard_map/reduce_scatter | solution.py:230
  430.0 263.9 %reduce-scatter.7.cloned.1.call-start = ((), (), s32[]{:S(2)}) async-start(), calls=%async_computation.5 | async-start | bytes 4718592 | tf_op jit(solution)/shard_map/reduce_scatter | solution.py:230
  440.3 345.3 %reduce-scatter.5.cloned.1.call-start = ((), (), s32[]{:S(2)}) async-start(), calls=%async_computation.4 | async-start | bytes 4718592 | tf_op jit(solution)/shard_map/reduce_scatter | solution.py:230
  450.9 1.9 copy-start.3
  450.9 3.5 copy-start.2
  785.5 2.2 copy-start
Sparse Core Ops, SparseCore 0:
  13.0 73.6 all-gather.14
  88.8 71.9 all-gather.12
  162.9 71.3 all-gather.10
  236.3 71.6 all-gather.16
  419.8 90.9 reduce-scatter.10
  514.3 87.9 reduce-scatter.8
  605.9 87.9 reduce-scatter.6
  697.5 87.9 reduce-scatter.4
